TPU v7x, 512 devices: a whole 4x4x16 slice. The times are simulated.
512 devices in a mesh: dp: 32 (over z, core), fsdp: 16 (over x, y).
Axes of the slice: x: 4, y: 4, z: 16, core: 2. Of those that a mesh axis runs over, the one named last changes fastest.
Arguments:
- gradients: bfloat16 [1, 8192, 28672], P(None, 'fsdp', 'dp'), may hold values from -16 to 16
- errors: bfloat16 [1, 8192, 28672], P(None, 'fsdp', 'dp'), may hold values from -4 to 4
- start_factor: float32 [1, 32, 28672], P(None, None, 'dp'), may hold values from -6 to 6
Outputs:
- compressed: bfloat16 [1, 8192, 28672], P(None, 'fsdp', 'dp')
- new_errors: bfloat16 [1, 8192, 28672], P(None, 'fsdp', 'dp')
All inputs are finite; a program needn't handle non-finite values.
Results may differ from a plain program's by a relative error of at most 0.0085.
Values sent between devices are 32-bit elements; how exact they have to be, the bound alone decides.
No kernel may reach another device: no remote copies, remote signals or barrier semaphores. Data moves between devices by JAX's collectives and lax.ppermute only.
A program may use at most 64 MiB of HBM per device.

v0:
```python
import jax
import jax.numpy as jnp
from jax import lax
from jax.sharding import PartitionSpec as P


def orthonormal(lower, columns):

    def solve_single(factor, right_side):
        return jax.scipy.linalg.solve_triangular(factor, right_side, lower=True)

    return jax.vmap(solve_single)(lower, columns)


def shards(gradients, errors, start_factor):
    combined = (gradients.astype(jnp.float32) + errors.astype(jnp.float32)).astype(jnp.bfloat16)
    factor_low = start_factor.astype(jnp.bfloat16)
    products = jnp.einsum("mrc,mdc->mrd", factor_low, combined, preferred_element_type=jnp.float32)
    summed = lax.psum(products, "dp")
    whole = lax.all_gather(summed, "fsdp", axis=2, tiled=True)
    gram = jnp.einsum(
        "mrd,msd->mrs",
        whole,
        whole,
        precision=lax.Precision.HIGHEST,
        preferred_element_type=jnp.float32,
    )
    lower = jnp.linalg.cholesky(gram)
    basis = orthonormal(lower, summed)
    basis_low = basis.astype(jnp.bfloat16)
    projected = jnp.einsum("mrd,mdc->mrc", basis_low, combined, preferred_element_type=jnp.float32)
    factor_new = lax.psum(projected, "fsdp")
    rebuilt = jnp.einsum(
        "mrd,mrc->mdc",
        basis,
        factor_new,
        precision=lax.Precision.HIGHEST,
        preferred_element_type=jnp.float32,
    )
    compressed = rebuilt.astype(jnp.bfloat16)
    new_errors = (combined.astype(jnp.float32) - rebuilt).astype(jnp.bfloat16)
    return (compressed, new_errors)


def solution(mesh):
    placed = (P(None, "fsdp", "dp"), P(None, "fsdp", "dp"), P(None, None, "dp"))
    return jax.shard_map(
        shards,
        mesh=mesh,
        in_specs=placed,
        out_specs=(P(None, "fsdp", "dp"), P(None, "fsdp", "dp")),
        check_vma=False,
    )
```

profile of v0, /device:TPU:32, one launch (start us, length us, event | category | flops | bytes accessed | tf_op | source)
XLA Modules:
  0.0 389.8 jit_solution(7160317326725971944)
XLA Ops:
  7.2 0.0 all-reduce.3.cloned.1.call-start
  7.2 0.0 copy-start.1
  7.2 2.5 convolution_bitcast_fusion
  9.8 0.0 copy-start
  9.8 0.0 all-reduce.3.cloned.1.call-update
  9.8 0.0 all-gather.2.cloned.1.call-start
  9.8 190.7 %all-reduce.3.cloned.1.call-done = f32[1,32,512]{2,1,0:T(8,128)} async-done(((f32[1,32,512]{2,1,0:T(8,128)}), f32[1,32,512]{2,1,0:T(8,128)}) %all-reduce.3.cloned.1.call-update) | async-done | bytes 65552 | tf_op jit(solution)/shard_map/psum | solution.py:19
  200.5 0.0 copy-start.2
  200.5 0.0 all-gather.2.cloned.1.call-update
  200.5 0.0 all-reduce.5.cloned.1.call-start
  200.6 54.9 %all-gather.2.cloned.1.call-done = f32[1,32,8192]{2,1,0:T(8,128)} async-done(((f32[1,32,512]{2,1,0:T(8,128)}), f32[1,32,8192]{2,1,0:T(8,128)}) %all-gather.2.cloned.1.call-update) | async-done | bytes 1048592 | tf_op jit(solution)/shard_map/all_gather | solution.py:20
  255.5 2.5 fusion.1
  258.0 0.1 copy.6
  258.1 2.9 custom-call.8
  261.1 0.6 compare_reduce_fusion
  261.7 0.7 fusion.11
  262.4 2.4 custom-call.9
  264.8 0.0 copy-done.2
  264.8 0.3 fusion.6
  265.1 0.0 copy-done.1
  265.1 0.0 copy-done
  265.1 1.0 fusion.3
  266.1 0.0 all-reduce.5.cloned.1.call-update
  266.1 113.3 %all-reduce.5.cloned.1.call-done = f32[32,896]{1,0:T(8,128)} async-done(((f32[32,896]{1,0:T(8,128)}), f32[32,896]{1,0:T(8,128)}) %all-reduce.5.cloned.1.call-update) | async-done | bytes 114704 | tf_op jit(solution)/shard_map/psum | solution.py:32
  379.4 3.9 fusion
  (2 shorter events, 0.0 us)
Async XLA Ops:
  7.2 193.3 %all-reduce.3.cloned.1.call-start = ((), (), s32[]{:S(2)}) async-start(), calls=%async_computation | async-start | bytes 131072 | tf_op jit(solution)/shard_map/psum | solution.py:19
  7.2 257.9 %copy-start.1 = (bf16[1,512,896]{2,1,0:T(8,128)(2,1)S(1)}, bf16[1,512,896]{2,1,0:T(8,128)(2,1)}, u32[]{:S(2)}) copy-start(bf16[1,512,896]{2,1,0:T(8,128)(2,1)} %param.3) | copy-start | bytes 2752516
  9.8 255.3 %copy-start = (bf16[1,512,896]{2,1,0:T(8,128)(2,1)S(1)}, bf16[1,512,896]{2,1,0:T(8,128)(2,1)}, u32[]{:S(2)}) copy-start(bf16[1,512,896]{2,1,0:T(8,128)(2,1)} %param.4) | copy-start | bytes 2752516
  9.8 245.7 %all-gather.2.cloned.1.call-start = ((), (), s32[]{:S(2)}) async-start(), calls=%async_computation.1 | async-start | bytes 1114112 | tf_op jit(solution)/shard_map/all_gather | solution.py:20
  200.5 64.3 %copy-start.2 = (f32[1,32,512]{2,1,0:T(8,128)S(1)}, f32[1,32,512]{2,1,0:T(8,128)}, u32[]{:S(2)}) copy-start(f32[1,32,512]{2,1,0:T(8,128)} %all-reduce.3.cloned.1.call-done) | copy-start | bytes 196612
  200.5 178.9 %all-reduce.5.cloned.1.call-start = ((), (), s32[]{:S(2)}) async-start(), calls=%async_computation.2 | async-start | bytes 229376 | tf_op jit(solution)/shard_map/psum | solution.py:32
Sparse Core Ops, SparseCore 0:
  10.9 189.5 all-reduce.2
  203.6 51.8 all-gather.1
  266.2 113.1 all-reduce.4
where the time goes:
time: 390 us
  waiting for transfers between devices  359 us (92%)
  between operations  13.8 us (4%)
  matrix products  10.2 us (3%)
  other arithmetic  6.69 us (2%)
    psum x1, waiting for transfers between devices, shards(): summed = lax.psum(products, 'dp')  191 us
    psum x1, waiting for transfers between devices, shards(): factor_new = lax.psum(projected, 'fsdp')  113 us
    all_gather x1, waiting for transfers between devices, shards(): whole = lax.all_gather(summed, 'fsdp', axis=2, tiled=True)  54.9 us
  transfers between devices with their start and end apart: 3, of which 3 were waited for; matrix products, arithmetic and copies ran while one was open for 0% of the time, Pallas kernels for 0%

commit v1 on v0

--- a/solution.py
+++ b/solution.py
@@ -29,7 +29,7 @@
     basis = orthonormal(lower, summed)
     basis_low = basis.astype(jnp.bfloat16)
     projected = jnp.einsum("mrd,mdc->mrc", basis_low, combined, preferred_element_type=jnp.float32)
-    factor_new = lax.psum(projected, "fsdp")
+    factor_new = jnp.sum(lax.all_gather(projected, "fsdp"), axis=0)
     rebuilt = jnp.einsum(
         "mrd,mrc->mdc",
         basis,

time: 390 us -> 338 us (0.87)
  the two profiles are of different devices: /device:TPU:32 before, /device:TPU:2 now
where the time goes in v1:
time: 338 us; the launch traced here: 337 us
  waiting for transfers between devices  305 us (90%)
  between operations  13.8 us (4%)
  matrix products  10.2 us (3%)
  other arithmetic  8.29 us (2%)
    psum x1, waiting for transfers between devices, shards(): summed = lax.psum(products, 'dp')  191 us
    all_gather x1, waiting for transfers between devices, shards(): factor_new = jnp.sum(lax.all_gather(projected, 'fsdp'), axis=0)  59.3 us
    all_gather x1, waiting for transfers between devices, shards(): whole = lax.all_gather(summed, 'fsdp', axis=2, tiled=True)  54.2 us
  transfers between devices with their start and end apart: 3, of which 3 were waited for; matrix products, arithmetic and copies ran while one was open for 0% of the time, Pallas kernels for 0%

profile of v1, /device:TPU:2, one launch (start us, length us, event | category | flops | bytes accessed | tf_op | source)
XLA Modules:
  0.0 337.4 jit_solution(15549703629740626446)
XLA Ops:
  7.2 0.0 copy-start
  7.2 0.0 copy-start.1
  7.2 0.0 all-reduce.2.cloned.1.call-start
  7.2 2.6 convolution_bitcast_fusion
  9.8 0.0 all-reduce.2.cloned.1.call-update
  9.8 0.0 all-gather.4.cloned.1.call-start
  9.9 191.4 %all-reduce.2.cloned.1.call-done = f32[1,32,512]{2,1,0:T(8,128)} async-done(((f32[1,32,512]{2,1,0:T(8,128)}), f32[1,32,512]{2,1,0:T(8,128)}) %all-reduce.2.cloned.1.call-update) | async-done | bytes 65552 | tf_op jit(solution)/shard_map/psum | solution.py:19
  201.3 0.0 all-gather.4.cloned.1.call-update
  201.3 0.0 all-gather.6.cloned.1.call-start
  201.4 54.2 %all-gather.4.cloned.1.call-done = f32[1,32,8192]{2,1,0:T(8,128)} async-done(((f32[1,32,512]{2,1,0:T(8,128)}), f32[1,32,8192]{2,1,0:T(8,128)}) %all-gather.4.cloned.1.call-update) | async-done | bytes 1048592 | tf_op jit(solution)/shard_map/all_gather | solution.py:20
  255.5 2.5 fusion.1
  258.1 0.1 copy.6
  258.1 2.9 custom-call.8
  261.1 0.6 compare_reduce_fusion
  261.7 0.7 fusion.11
  262.4 2.4 custom-call.9
  264.8 1.1 fusion.6
  266.0 0.0 copy-done
  266.0 0.0 copy-done.1
  266.0 1.0 fusion.3
  267.0 0.0 all-gather.6.cloned.1.call-update
  267.0 59.3 %all-gather.6.cloned.1.call-done = f32[512,896]{1,0:T(8,128)} async-done(((f32[32,896]{1,0:T(8,128)}), f32[512,896]{1,0:T(8,128)}) %all-gather.6.cloned.1.call-update) | async-done | bytes 1835024 | tf_op jit(solution)/shard_map/all_gather | solution.py:32
  326.3 1.6 reduce.10
  327.9 3.0 fusion
  (2 shorter events, 0.0 us)
Async XLA Ops:
  7.2 258.8 %copy-start = (bf16[1,512,896]{2,1,0:T(8,128)(2,1)S(1)}, bf16[1,512,896]{2,1,0:T(8,128)(2,1)}, u32[]{:S(2)}) copy-start(bf16[1,512,896]{2,1,0:T(8,128)(2,1)} %param.4) | copy-start | bytes 2752516
  7.2 258.8 %copy-start.1 = (bf16[1,512,896]{2,1,0:T(8,128)(2,1)S(1)}, bf16[1,512,896]{2,1,0:T(8,128)(2,1)}, u32[]{:S(2)}) copy-start(bf16[1,512,896]{2,1,0:T(8,128)(2,1)} %param.3) | copy-start | bytes 2752516
  7.2 194.1 %all-reduce.2.cloned.1.call-start = ((), (), s32[]{:S(2)}) async-start(), calls=%async_computation | async-start | bytes 131072 | tf_op jit(solution)/shard_map/psum | solution.py:19
  9.8 245.7 %all-gather.4.cloned.1.call-start = ((), (), s32[]{:S(2)}) async-start(), calls=%async_computation.1 | async-start | bytes 1114112 | tf_op jit(solution)/shard_map/all_gather | solution.py:20
  201.3 125.0 %all-gather.6.cloned.1.call-start = ((), (), s32[]{:S(2)}) async-start(), calls=%async_computation.2 | async-start | bytes 1949696 | tf_op jit(solution)/shard_map/all_gather | solution.py:32
Sparse Core Ops, SparseCore 0:
  10.9 190.3 all-reduce.1
  204.4 51.1 all-gather.3
  267.1 59.1 all-gather.5
